TPU v7x, 32 devices: a whole 2x2x4 slice. The times are simulated.
32 devices in a mesh: expert: 8 (over z, x), tensor: 4 (over y, core).
Axes of the slice: x: 2, y: 2, z: 4, core: 2. Of those that a mesh axis runs over, the one named last changes fastest.
Arguments:
- tokens: bfloat16 [1024, 4096], P('expert', 'tensor'), may hold values from -6 to 6
- expert_ids: int32 [1024, 8], P('expert'), may hold values from 0 to 15, all different within a row; in each aligned block of 128 rows (0 to 127, 128 to 255, ...) at most 96 rows name the same one
- combine_weight: float32 [1024, 8], P('expert'), may hold values from 0.05 to 0.5
- gate_weight: bfloat16 [16, 4096, 1024], P('expert', 'tensor'), may hold values from -0.09375 to 0.09375
- up_weight: bfloat16 [16, 4096, 1024], P('expert', 'tensor'), may hold values from -0.09375 to 0.09375
- down_weight: bfloat16 [16, 1024, 4096], P('expert', None, 'tensor'), may hold values from -0.1875 to 0.1875
- out_cotangent: bfloat16 [1024, 4096], P('expert', 'tensor'), may hold values from -3 to 3
Outputs:
- mixed: bfloat16 [1024, 4096], P('expert', 'tensor')
- token_grad: bfloat16 [1024, 4096], P('expert', 'tensor')
- combine_grad: float32 [1024, 8], P('expert')
- gate_grad: bfloat16 [16, 4096, 1024], P('expert', 'tensor')
- up_grad: bfloat16 [16, 4096, 1024], P('expert', 'tensor')
- down_grad: bfloat16 [16, 1024, 4096], P('expert', None, 'tensor')
Inputs may be any that keep to these rules, and one draw needn't show every extreme that they name: `expert_ids`: each row names 8 different experts. Among the rows of one device no expert is named by more than 96 rows, a bound that some block reaches.
All inputs are finite; a program needn't handle non-finite values.
Results may differ from a plain program's by a relative error of at most 0.023.
Values may be sent and summed in bfloat16 or wider, within the bound.
A program may use at most 128 MiB of HBM per device.

v0:
```python
import jax
import jax.numpy as jnp
from jax import lax
from jax.sharding import PartitionSpec as P

F32, BF16 = (jnp.float32, jnp.bfloat16)


def dot(form, left, right):
    return jnp.einsum(form, left, right, preferred_element_type=F32)


def per_device(
    tokens, expert_ids, combine_weight, gate_weight, up_weight, down_weight, out_cotangent
):
    groups = lax.axis_size("expert")
    shards = lax.axis_size("tensor")
    local = gate_weight.shape[0]
    width = tokens.shape[1]
    hidden = gate_weight.shape[2]
    rows = tokens.shape[0]
    top = expert_ids.shape[1]
    experts = local * groups
    capacity = 3 * rows * top // (2 * experts)
    slots = groups * capacity
    total = local * slots
    own = total // shards
    mine = lax.axis_index("expert")
    named = expert_ids[:, :, None] == jnp.arange(experts, dtype=jnp.int32)
    dense_weight = jnp.sum(jnp.where(named, combine_weight[:, :, None], 0.0), axis=1)
    weights_all = lax.all_gather(dense_weight, "expert", axis=0)
    tokens_all = lax.all_gather(tokens, "expert", axis=0)
    cotangent_all = lax.all_gather(out_cotangent, "expert", axis=0)
    weight_tok = lax.dynamic_slice_in_dim(weights_all, mine * local, local, 2)
    weight_tok = weight_tok.transpose(2, 0, 1)
    served = weight_tok > 0.0
    earlier = (jnp.arange(rows)[:, None] < jnp.arange(rows)[None, :]).astype(BF16)
    position = dot("ebs,st->ebt", served.astype(BF16), earlier)
    at_slot = jnp.where(served, position, -1.0).astype(jnp.int32)
    chosen = at_slot[:, :, None, :] == jnp.arange(capacity, dtype=jnp.int32)[:, None]
    place = chosen.astype(BF16)
    weight_slot = jnp.sum(jnp.where(chosen, weight_tok[:, :, None, :], 0.0), axis=3)
    weight_slot = weight_slot.reshape(total, 1)
    weight_own = lax.dynamic_slice_in_dim(weight_slot, lax.axis_index("tensor") * own, own, 0)

    def dispatch(values):
        return [
            dot("bct,btd->bcd", place[e], values).astype(BF16).reshape(slots, width)
            for e in range(local)
        ]

    def scatter_rows(parts):
        return lax.psum_scatter(
            jnp.concatenate(parts, axis=0), "tensor", scatter_dimension=0, tiled=True
        ).astype(F32)

    def gather_rows(value):
        full = lax.all_gather(value.astype(BF16), "tensor", axis=0, tiled=True)
        return full.reshape(local, slots, hidden)

    def combine(parts):
        total_sum = sum(
            (
                dot("bct,bcd->btd", place[e], parts[e].reshape(groups, capacity, width))
                for e in range(local)
            )
        )
        return lax.psum_scatter(
            total_sum.astype(BF16), "expert", scatter_dimension=0, tiled=True
        ).reshape(rows, width)

    routed = dispatch(tokens_all)
    gate = scatter_rows(
        [dot("cd,dk->ck", routed[e], gate_weight[e]).astype(BF16) for e in range(local)]
    )
    up = scatter_rows(
        [dot("cd,dk->ck", routed[e], up_weight[e]).astype(BF16) for e in range(local)]
    )
    incoming = dispatch(cotangent_all)
    pulled = scatter_rows(
        [dot("cd,kd->ck", incoming[e], down_weight[e]).astype(BF16) for e in range(local)]
    )
    sigma = jax.nn.sigmoid(gate)
    silu = gate * sigma
    act = silu * up
    weighted_act = gather_rows(weight_own * act)
    weighted_pull = weight_own * pulled
    gate_diff = gather_rows(weighted_pull * up * sigma * (1.0 + gate * (1.0 - sigma)))
    up_diff = gather_rows(weighted_pull * silu)
    pair_own = jnp.sum(act * pulled, axis=1)
    pair_all = lax.all_gather(pair_own, "tensor", axis=0, tiled=True)
    pair_all = pair_all.reshape(local, groups, capacity)
    pair_tok = jnp.sum(jnp.where(chosen, pair_all[:, :, :, None], 0.0), axis=2)
    pair_tok = lax.all_to_all(
        pair_tok.transpose(1, 0, 2), "expert", split_axis=0, concat_axis=0, tiled=True
    ).reshape(experts, rows)
    combine_grad = jnp.sum(jnp.where(named, pair_tok.T[:, None, :], 0.0), axis=2)
    mixed = combine(
        [dot("ck,kd->cd", weighted_act[e], down_weight[e]).astype(BF16) for e in range(local)]
    )
    token_grad = combine(
        [
            (
                dot("ck,dk->cd", gate_diff[e], gate_weight[e])
                + dot("ck,dk->cd", up_diff[e], up_weight[e])
            ).astype(BF16)
            for e in range(local)
        ]
    )
    down_grad = jnp.stack(
        [dot("ck,cd->kd", weighted_act[e], incoming[e]).astype(BF16) for e in range(local)]
    )
    gate_grad = jnp.stack(
        [dot("cd,ck->dk", routed[e], gate_diff[e]).astype(BF16) for e in range(local)]
    )
    up_grad = jnp.stack(
        [dot("cd,ck->dk", routed[e], up_diff[e]).astype(BF16) for e in range(local)]
    )
    return (mixed, token_grad, combine_grad, gate_grad, up_grad, down_grad)


def solution(mesh):
    wide, narrow = (P("expert", "tensor"), P("expert", None))
    deep, flat = (P("expert", "tensor", None), P("expert", None, "tensor"))
    return jax.shard_map(
        per_device,
        mesh=mesh,
        in_specs=(wide, narrow, narrow, deep, deep, flat, wide),
        out_specs=(wide, wide, narrow, deep, deep, flat),
        check_vma=False,
    )
```

profile of v0, /device:TPU:0, one launch (start us, length us, event | category | flops | bytes accessed | tf_op | source)
XLA Modules:
  0.0 485.3 jit_solution(2494550937460764869)
XLA Ops:
  9.4 32.6 %all-gather = f32[1024,16]{0,1:T(8,128)S(1)} all-gather(f32[128,16]{0,1:T(8,128)S(1)} %select_reduce_fusion.3), channel_id=2, replica_groups=mesh['expert'=8,'tensor'=4] {'expert'}, dimensions={0}, use_global_device_ids=true | all-gather | bytes 73728 | tf_op jit(solution)/shard_map/all_gather | solution.py:31
  42.3 20.0 %all-gather.16.cloned.1.call-done = bf16[1024,1024]{1,0:T(8,128)(2,1)} async-done(((bf16[128,1024]{1,0:T(8,128)(2,1)}), bf16[1024,1024]{1,0:T(8,128)(2,1)}) %all-gather.16.cloned.1.call-update) | async-done | bytes 2097168 | tf_op jit(solution)/shard_map/all_gather | solution.py:32
  71.7 40.4 %all-gather.18.cloned.1.call-done = bf16[1024,1024]{1,0:T(8,128)(2,1)} async-done(((bf16[128,1024]{1,0:T(8,128)(2,1)}), bf16[1024,1024]{1,0:T(8,128)(2,1)}) %all-gather.18.cloned.1.call-update) | async-done | bytes 2097168 | tf_op jit(solution)/shard_map/all_gather | solution.py:33
  112.1 2.3 convolution_convert_fusion
  122.0 3.7 fusion.40
  129.6 22.1 %reduce-scatter.8.cloned.1.call-done = bf16[384,1024]{1,0:T(8,128)(2,1)} async-done(((bf16[1536,1024]{1,0:T(8,128)(2,1)}), bf16[384,1024]{1,0:T(8,128)(2,1)}) %reduce-scatter.8.cloned.1.call-update) | async-done | bytes 786448 | tf_op jit(solution)/shard_map/reduce_scatter | solution.py:53
  151.6 40.9 %reduce-scatter.12.cloned.1.call-done = bf16[384,1024]{1,0:T(8,128)(2,1)} async-done(((bf16[1536,1024]{1,0:T(8,128)(2,1)}), bf16[384,1024]{1,0:T(8,128)(2,1)}) %reduce-scatter.12.cloned.1.call-update) | async-done | bytes 786448 | tf_op jit(solution)/shard_map/reduce_scatter | solution.py:53
  192.5 40.9 %reduce-scatter.6.cloned.1.call-done = bf16[384,1024]{1,0:T(8,128)(2,1)} async-done(((bf16[1536,1024]{1,0:T(8,128)(2,1)}), bf16[384,1024]{1,0:T(8,128)(2,1)}) %reduce-scatter.6.cloned.1.call-update) | async-done | bytes 786448 | tf_op jit(solution)/shard_map/reduce_scatter | solution.py:53
  233.4 2.3 fusion.65
  235.7 5.2 %all-gather.3 = f32[4,1,384]{2,1,0:T(1,128)S(1)} all-gather(f32[1,1,384]{2,1,0:T(1,128)S(1)} %reshape.84), channel_id=1, replica_groups=mesh['expert'=8,'tensor'=4] {'tensor'}, dimensions={0}, use_global_device_ids=true | all-gather | bytes 7680 | tf_op jit(solution)/shard_map/all_gather | solution.py:91
  241.8 2.6 fusion.64
  245.9 27.1 %all-gather.10.cloned.1.call-done = bf16[1536,1024]{1,0:T(8,128)(2,1)} async-done(((bf16[384,1024]{1,0:T(8,128)(2,1)}), bf16[1536,1024]{1,0:T(8,128)(2,1)}) %all-gather.10.cloned.1.call-update) | async-done | bytes 3145744 | tf_op jit(solution)/shard_map/all_gather | solution.py:58
  273.0 4.0 fusion.49
  283.3 20.3 %all-gather.14.cloned.1.call-done = bf16[1536,1024]{1,0:T(8,128)(2,1)} async-done(((bf16[384,1024]{1,0:T(8,128)(2,1)}), bf16[1536,1024]{1,0:T(8,128)(2,1)}) %all-gather.14.cloned.1.call-update) | async-done | bytes 3145744 | tf_op jit(solution)/shard_map/all_gather | solution.py:58
  303.7 3.9 fusion.12
  307.6 26.8 %all-gather.12.cloned.1.call-done = bf16[1536,1024]{1,0:T(8,128)(2,1)} async-done(((bf16[384,1024]{1,0:T(8,128)(2,1)}), bf16[1536,1024]{1,0:T(8,128)(2,1)}) %all-gather.12.cloned.1.call-update) | async-done | bytes 3145744 | tf_op jit(solution)/shard_map/all_gather | solution.py:58
  334.3 4.1 add_convert_fusion.3
  347.9 12.2 %all_to_all.5 = f32[8,2,128]{2,1,0:T(2,128)S(1)} all-to-all(f32[8,2,128]{2,1,0:T(2,128)S(1)} %copy.26), channel_id=1, replica_groups=mesh['expert'=8,'tensor'=4] {'expert'}, dimensions={0} | all-to-all | bytes 16384 | tf_op jit(solution)/shard_map/all_to_all | solution.py:94
  360.7 3.4 convert_bitcast_fusion.4
  366.0 2.5 pad_maximum_fusion
  373.1 2.5 pad_maximum_fusion.1
  380.7 2.4 pad_maximum_fusion.2
  383.1 23.7 %reduce-scatter.10.cloned.1.call-done = bf16[1,128,1024]{2,1,0:T(8,128)(2,1)} async-done(((bf16[8,128,1024]{2,1,0:T(8,128)(2,1)}), bf16[1,128,1024]{2,1,0:T(8,128)(2,1)}) %reduce-scatter.10.cloned.1.call-update) | async-done | bytes 262160 | tf_op jit(solution)/shard_map/reduce_scatter | solution.py:68
  406.8 71.4 %reduce-scatter.14.cloned.1.call-done = bf16[1,128,1024]{2,1,0:T(8,128)(2,1)} async-done(((bf16[8,128,1024]{2,1,0:T(8,128)(2,1)}), bf16[1,128,1024]{2,1,0:T(8,128)(2,1)}) %reduce-scatter.14.cloned.1.call-update) | async-done | bytes 262160 | tf_op jit(solution)/shard_map/reduce_scatter | solution.py:68
  (108 shorter events, 53.4 us)
Async XLA Ops:
  7.2 55.1 %all-gather.16.cloned.1.call-start = ((), (), s32[]{:S(2)}) async-start(), calls=%async_computation.14 | async-start | bytes 2359296 | tf_op jit(solution)/shard_map/all_gather | solution.py:32
  7.9 104.2 %all-gather.18.cloned.1.call-start = ((), (), s32[]{:S(2)}) async-start(), calls=%async_computation.15 | async-start | bytes 2359296 | tf_op jit(solution)/shard_map/all_gather | solution.py:33
  8.6 143.0 %reduce-scatter.8.cloned.1.call-start = ((), (), s32[]{:S(2)}) async-start(), calls=%async_computation.7 | async-start | bytes 3932160 | tf_op jit(solution)/shard_map/reduce_scatter | solution.py:53
  62.3 3.8 copy-start.16
  64.6 57.4 %copy-start.7 = (bf16[8,96,1024]{2,1,0:T(8,128)(2,1)}, bf16[8,96,1024]{2,1,0:T(8,128)(2,1)S(1)}, u32[]{:S(2)}) copy-start(bf16[8,96,1024]{2,1,0:T(8,128)(2,1)S(1)} %convolution_convert_fusion.2) | copy-start | bytes 4718596
  65.2 60.5 %copy-start.5 = (bf16[8,96,1024]{2,1,0:T(8,128)(2,1)}, bf16[8,96,1024]{2,1,0:T(8,128)(2,1)S(1)}, u32[]{:S(2)}) copy-start(bf16[8,96,1024]{2,1,0:T(8,128)(2,1)S(1)} %convolution_convert_fusion.3) | copy-start | bytes 4718596
  71.6 120.9 %reduce-scatter.12.cloned.1.call-start = ((), (), s32[]{:S(2)}) async-start(), calls=%async_computation.10 | async-start | bytes 3932160 | tf_op jit(solution)/shard_map/reduce_scatter | solution.py:53
  112.1 3.7 copy-start.14
  121.5 111.9 %reduce-scatter.6.cloned.1.call-start = ((), (), s32[]{:S(2)}) async-start(), calls=%async_computation.6 | async-start | bytes 3932160 | tf_op jit(solution)/shard_map/reduce_scatter | solution.py:53
  122.0 3.7 copy-start.18
  129.5 143.5 %all-gather.10.cloned.1.call-start = ((), (), s32[]{:S(2)}) async-start(), calls=%async_computation.8 | async-start | bytes 3932160 | tf_op jit(solution)/shard_map/all_gather | solution.py:58
  151.6 90.1 %copy-start.2 = (bf16[384,1024]{1,0:T(8,128)(2,1)S(1)}, bf16[384,1024]{1,0:T(8,128)(2,1)}, u32[]{:S(2)}) copy-start(bf16[384,1024]{1,0:T(8,128)(2,1)} %reduce-scatter.8.cloned.1.call-done) | copy-start | bytes 2359300
  192.5 49.2 %copy-start.3 = (bf16[384,1024]{1,0:T(8,128)(2,1)S(1)}, bf16[384,1024]{1,0:T(8,128)(2,1)}, u32[]{:S(2)}) copy-start(bf16[384,1024]{1,0:T(8,128)(2,1)} %reduce-scatter.12.cloned.1.call-done) | copy-start | bytes 2359300
  233.4 8.3 %copy-start.4 = (bf16[384,1024]{1,0:T(8,128)(2,1)S(1)}, bf16[384,1024]{1,0:T(8,128)(2,1)}, u32[]{:S(2)}) copy-start(bf16[384,1024]{1,0:T(8,128)(2,1)} %reduce-scatter.6.cloned.1.call-done) | copy-start | bytes 2359300
  244.3 59.3 %all-gather.14.cloned.1.call-start = ((), (), s32[]{:S(2)}) async-start(), calls=%async_computation.12 | async-start | bytes 3932160 | tf_op jit(solution)/shard_map/all_gather | solution.py:58
  245.1 89.2 %all-gather.12.cloned.1.call-start = ((), (), s32[]{:S(2)}) async-start(), calls=%async_computation.11 | async-start | bytes 3932160 | tf_op jit(solution)/shard_map/all_gather | solution.py:58
  245.8 161.0 %reduce-scatter.10.cloned.1.call-start = ((), (), s32[]{:S(2)}) async-start(), calls=%async_computation.9 | async-start | bytes 2359296 | tf_op jit(solution)/shard_map/reduce_scatter | solution.py:68
  273.0 4.8 copy-start.20
  283.1 195.1 %reduce-scatter.14.cloned.1.call-start = ((), (), s32[]{:S(2)}) async-start(), calls=%async_computation.13 | async-start | bytes 2359296 | tf_op jit(solution)/shard_map/reduce_scatter | solution.py:68
  334.3 4.9 copy-start.22
  347.8 12.2 %copy-start.13 = (s32[128,8]{0,1:T(8,128)S(1)}, s32[128,8]{0,1:T(8,128)}, u32[]{:S(2)}) copy-start(s32[128,8]{0,1:T(8,128)} %param.8) | copy-start | bytes 12292
  347.8 12.8 %copy-start.8 = (bf16[8,96,1024]{2,1,0:T(8,128)(2,1)S(1)}, bf16[8,96,1024]{2,1,0:T(8,128)(2,1)}, u32[]{:S(2)}) copy-start(bf16[8,96,1024]{2,1,0:T(8,128)(2,1)} %copy-done.7) | copy-start | bytes 4718596
  360.7 3.4 copy-start.25
  373.1 3.9 copy-start.21
  (12 other events, 31.5 us)
Sparse Core Ops, SparseCore 0:
  10.1 52.1 all-gather.15
  64.4 47.6 all-gather.17
  115.2 36.4 reduce-scatter.7
  154.6 37.8 reduce-scatter.11
  195.5 37.8 reduce-scatter.5
  244.5 28.4 all-gather.9
  275.1 28.4 all-gather.13
  305.8 28.4 all-gather.11
  338.4 68.3 reduce-scatter.9
  410.8 67.3 reduce-scatter.13
where the time goes:
time: 492 us; the launch traced here: 485 us
  waiting for transfers between devices  336 us (68%)
  matrix products  54.6 us (11%)
  blocking collectives  49.9 us (10%)
  other arithmetic  20.2 us (4%)
  between operations  14.8 us (3%)
  local copies, waits for them, and re-layouts  8.33 us (2%)
    reduce_scatter x3, waiting for transfers between devices, scatter_rows(): lax.psum_scatter(jnp.concatenate(parts, axis=0), 'tensor', scatter_dimens...  104 us
    reduce_scatter x2, waiting for transfers between devices, combine(): lax.psum_scatter(total_sum.astype(BF16), 'expert', scatter_dimension=0, t...  95.1 us
    all_gather x3, waiting for transfers between devices, gather_rows(): full = lax.all_gather(value.astype(BF16), 'tensor', axis=0, tiled=True)  74.2 us
    dot_general x27, matrix products, dot(): return jnp.einsum(form, left, right, preferred_element_type=F32)  54.6 us
    all_gather x1, waiting for transfers between devices, per_device(): cotangent_all = lax.all_gather(out_cotangent, 'expert', axis=0)  40.4 us
    all_gather x1, blocking collectives, per_device(): weights_all = lax.all_gather(dense_weight, 'expert', axis=0)  32.6 us
    all_gather x1, waiting for transfers between devices, per_device(): tokens_all = lax.all_gather(tokens, 'expert', axis=0)  20 us
    all_to_all x1, blocking collectives, per_device(): lax.all_to_all(pair_tok.transpose(1, 0, 2), 'expert', split_axis=0, conca...  12.2 us
  transfers between devices with their start and end apart: 10, of which 10 were waited for; matrix products, arithmetic and copies ran while one was open for 14% of the time, Pallas kernels for 0%

commit v1 on v0

--- a/solution.py
+++ b/solution.py
@@ -4,6 +4,12 @@
 from jax.sharding import PartitionSpec as P
 
 F32, BF16 = (jnp.float32, jnp.bfloat16)
+
+
+def joined_along(pieces, dim):
+    pieces = jnp.moveaxis(pieces, 0, dim)
+    lengths = pieces.shape
+    return pieces.reshape(*lengths[:dim], lengths[dim] * lengths[dim + 1], *lengths[dim + 2 :])
 
 
 def dot(form, left, right):
@@ -55,7 +61,20 @@
         ).astype(F32)
 
     def gather_rows(value):
-        full = lax.all_gather(value.astype(BF16), "tensor", axis=0, tiled=True)
+        shard = value.astype(BF16)
+        size = lax.axis_size("tensor")
+        pairs = [(i, (i + 1) % size) for i in range(size)]
+        back = [(b, a) for a, b in pairs]
+        lower, upper = ([], [])
+        for lap in range(size - 1):
+            if lap % 2 == 0:
+                lower.append(lax.ppermute(lower[-1] if lower else shard, "tensor", pairs))
+            else:
+                upper.append(lax.ppermute(upper[-1] if upper else shard, "tensor", back))
+        blocks = jnp.stack([*lower[::-1], shard, *upper])
+        shift = lax.axis_index("tensor") - len(lower)
+        blocks = blocks[(jnp.arange(size) - shift) % size]
+        full = joined_along(blocks, 0)
         return full.reshape(local, slots, hidden)
 
     def combine(parts):

time: 492 us -> 476 us (0.967)
  waiting for transfers between devices: 336 us -> 301 us
  local copies, waits for them, and re-layouts: 8.33 us -> 22.9 us
  matrix products: 54.6 us -> 46.4 us
  other arithmetic: 20.2 us -> 27.4 us
    all_gather x3 -> x0, waiting for transfers between devices: 74.2 us -> none  [gather_rows(): full = lax.all_gather(value.astype(BF16), 'tensor', axis=0, tiled=True)]
    ppermute x0 -> x9, waiting for transfers between devices: none -> 57 us  [the longest x6 57 us: gather_rows(): lower.append(lax.ppermute(lower[-1] if lower else shard, 'tensor', pairs))]
    reduce_scatter x2, waiting for transfers between devices: 95.1 us -> 78.3 us  [combine(): lax.psum_scatter(total_sum.astype(BF16), 'expert', scatter_dimension=0, t...]
    gather x0 -> x3, local copies, waits for them, and re-layouts: none -> 9.35 us  [gather_rows(): blocks = blocks[(jnp.arange(size) - shift) % size]]
    dot_general x27, matrix products: 54.6 us -> 46.4 us  [dot(): return jnp.einsum(form, left, right, preferred_element_type=F32)]
    another operation x1 -> x3, other arithmetic: 2.5 us -> 8.62 us  [gather_rows(): blocks = jnp.stack([*lower[::-1], shard, *upper])]
    unnamed x54 -> x76, local copies, waits for them, and re-layouts: 8.13 us -> 10.3 us
  transfers between devices with their start and end apart: 10 -> 16, of which waited for: 10 -> 11; matrix products, arithmetic and copies ran while one was open for 14% -> 17% of each run, Pallas kernels for 0% -> 0%
where the time goes in v1:
time: 476 us; the launch traced here: 468 us
  waiting for transfers between devices  301 us (63%)
  blocking collectives  49.8 us (10%)
  matrix products  46.4 us (10%)
  other arithmetic  27.4 us (6%)
  local copies, waits for them, and re-layouts  22.9 us (5%)
  between operations  14.9 us (3%)
  starting transfers between devices  5.84 us (1%)
    reduce_scatter x3, waiting for transfers between devices, scatter_rows(): lax.psum_scatter(jnp.concatenate(parts, axis=0), 'tensor', scatter_dimens...  104 us
    reduce_scatter x2, waiting for transfers between devices, combine(): lax.psum_scatter(total_sum.astype(BF16), 'expert', scatter_dimension=0, t...  78.3 us
    ppermute x6, waiting for transfers between devices, gather_rows(): lower.append(lax.ppermute(lower[-1] if lower else shard, 'tensor', pairs))  57 us
    dot_general x27, matrix products, dot(): return jnp.einsum(form, left, right, preferred_element_type=F32)  46.4 us
    all_gather x1, waiting for transfers between devices, per_device(): cotangent_all = lax.all_gather(out_cotangent, 'expert', axis=0)  40.4 us
    all_gather x1, blocking collectives, per_device(): weights_all = lax.all_gather(dense_weight, 'expert', axis=0)  32.6 us
    all_gather x1, waiting for transfers between devices, per_device(): tokens_all = lax.all_gather(tokens, 'expert', axis=0)  20 us
    all_to_all x1, blocking collectives, per_device(): lax.all_to_all(pair_tok.transpose(1, 0, 2), 'expert', split_axis=0, conca...  12.1 us
  transfers between devices with their start and end apart: 16, of which 11 were waited for; matrix products, arithmetic and copies ran while one was open for 17% of the time, Pallas kernels for 0%

profile of v1, /device:TPU:0, one launch (start us, length us, event | category | flops | bytes accessed | tf_op | source)
XLA Modules:
  0.0 468.3 jit_solution(10603589553037012394)
XLA Ops:
  9.4 32.6 %all-gather = f32[1024,16]{0,1:T(8,128)S(1)} all-gather(f32[128,16]{0,1:T(8,128)S(1)} %select_reduce_fusion.3), channel_id=2, replica_groups=mesh['expert'=8,'tensor'=4] {'expert'}, dimensions={0}, use_global_device_ids=true | all-gather | bytes 73728 | tf_op jit(solution)/shard_map/all_gather | solution.py:37
  42.3 20.0 %all-gather.7.cloned.1.call-done = bf16[1024,1024]{1,0:T(8,128)(2,1)} async-done(((bf16[128,1024]{1,0:T(8,128)(2,1)}), bf16[1024,1024]{1,0:T(8,128)(2,1)}) %all-gather.7.cloned.1.call-update) | async-done | bytes 2097168 | tf_op jit(solution)/shard_map/all_gather | solution.py:38
  71.7 40.4 %all-gather.9.cloned.1.call-done = bf16[1024,1024]{1,0:T(8,128)(2,1)} async-done(((bf16[128,1024]{1,0:T(8,128)(2,1)}), bf16[1024,1024]{1,0:T(8,128)(2,1)}) %all-gather.9.cloned.1.call-update) | async-done | bytes 2097168 | tf_op jit(solution)/shard_map/all_gather | solution.py:39
  122.1 3.6 fusion.40
  129.6 22.1 %reduce-scatter.8.cloned.1.call-done = bf16[384,1024]{1,0:T(8,128)(2,1)} async-done(((bf16[1536,1024]{1,0:T(8,128)(2,1)}), bf16[384,1024]{1,0:T(8,128)(2,1)}) %reduce-scatter.8.cloned.1.call-update) | async-done | bytes 786448 | tf_op jit(solution)/shard_map/reduce_scatter | solution.py:59
  151.7 40.9 %reduce-scatter.12.cloned.1.call-done = bf16[384,1024]{1,0:T(8,128)(2,1)} async-done(((bf16[1536,1024]{1,0:T(8,128)(2,1)}), bf16[384,1024]{1,0:T(8,128)(2,1)}) %reduce-scatter.12.cloned.1.call-update) | async-done | bytes 786448 | tf_op jit(solution)/shard_map/reduce_scatter | solution.py:59
  192.5 40.9 %reduce-scatter.6.cloned.1.call-done = bf16[384,1024]{1,0:T(8,128)(2,1)} async-done(((bf16[1536,1024]{1,0:T(8,128)(2,1)}), bf16[384,1024]{1,0:T(8,128)(2,1)}) %reduce-scatter.6.cloned.1.call-update) | async-done | bytes 786448 | tf_op jit(solution)/shard_map/reduce_scatter | solution.py:59
  235.7 5.2 %all-gather.3 = f32[4,1,384]{2,1,0:T(1,128)S(1)} all-gather(f32[1,1,384]{2,1,0:T(1,128)S(1)} %reshape.154), channel_id=1, replica_groups=mesh['expert'=8,'tensor'=4] {'tensor'}, dimensions={0}, use_global_device_ids=true | all-gather | bytes 7680 | tf_op jit(solution)/shard_map/all_gather | solution.py:110
  246.3 17.0 %collective-permute-done = bf16[384,1024]{1,0:T(8,128)(2,1)S(1)} collective-permute-done((bf16[384,1024]{1,0:T(8,128)(2,1)S(1)}, bf16[384,1024]{1,0:T(8,128)(2,1)S(1)}, u32[]{:S(2)}, u32[]{:S(2)}) %collective-permute-start) | collective-permute-done | bytes 786464 | tf_op jit(solution)/shard_map/ppermute | solution.py:71
  266.1 12.9 %collective-permute-done.6 = bf16[384,1024]{1,0:T(8,128)(2,1)} collective-permute-done((bf16[384,1024]{1,0:T(8,128)(2,1)}, bf16[384,1024]{1,0:T(8,128)(2,1)}, u32[]{:S(2)}, u32[]{:S(2)}) %collective-permute-start.6) | collective-permute-done | bytes 786464 | tf_op jit(solution)/shard_map/ppermute | solution.py:71
  279.0 16.8 %collective-permute-done.3 = bf16[384,1024]{1,0:T(8,128)(2,1)} collective-permute-done((bf16[384,1024]{1,0:T(8,128)(2,1)}, bf16[384,1024]{1,0:T(8,128)(2,1)}, u32[]{:S(2)}, u32[]{:S(2)}) %collective-permute-start.3) | collective-permute-done | bytes 786464 | tf_op jit(solution)/shard_map/ppermute | solution.py:71
  295.9 10.2 %collective-permute-done.1 = bf16[384,1024]{1,0:T(8,128)(2,1)S(1)} collective-permute-done((bf16[384,1024]{1,0:T(8,128)(2,1)S(1)}, bf16[384,1024]{1,0:T(8,128)(2,1)S(1)}, u32[]{:S(2)}, u32[]{:S(2)}) %collective-permute-start.1) | collective-permute-done | bytes 786464 | tf_op jit(solution)/shard_map/ppermute | solution.py:71
  309.0 2.4 gather_fusion
  311.4 2.4 fusion.86
  321.3 3.2 pad_maximum_fusion.8
  324.6 2.6 gather_fusion.2
  327.2 3.4 pad_maximum_fusion.7
  330.6 4.3 gather_fusion.1
  338.5 2.8 copy-done.34
  352.0 12.1 %all_to_all.5 = f32[8,2,128]{2,1,0:T(2,128)S(1)} all-to-all(f32[8,2,128]{2,1,0:T(2,128)S(1)} %copy.26), channel_id=1, replica_groups=mesh['expert'=8,'tensor'=4] {'expert'}, dimensions={0} | all-to-all | bytes 16384 | tf_op jit(solution)/shard_map/all_to_all | solution.py:113
  368.5 2.4 pad_maximum_fusion.2
  379.2 3.7 pad_maximum_fusion
  382.9 6.8 %reduce-scatter.10.cloned.1.call-done = bf16[1,128,1024]{2,1,0:T(8,128)(2,1)} async-done(((bf16[8,128,1024]{2,1,0:T(8,128)(2,1)}), bf16[1,128,1024]{2,1,0:T(8,128)(2,1)}) %reduce-scatter.10.cloned.1.call-update) | async-done | bytes 262160 | tf_op jit(solution)/shard_map/reduce_scatter | solution.py:87
  389.7 71.5 %reduce-scatter.14.cloned.1.call-done = bf16[1,128,1024]{2,1,0:T(8,128)(2,1)} async-done(((bf16[8,128,1024]{2,1,0:T(8,128)(2,1)}), bf16[1,128,1024]{2,1,0:T(8,128)(2,1)}) %reduce-scatter.14.cloned.1.call-update) | async-done | bytes 262160 | tf_op jit(solution)/shard_map/reduce_scatter | solution.py:87
  (149 shorter events, 73.2 us)
Async XLA Ops:
  7.2 55.1 %all-gather.7.cloned.1.call-start = ((), (), s32[]{:S(2)}) async-start(), calls=%async_computation.11 | async-start | bytes 2359296 | tf_op jit(solution)/shard_map/all_gather | solution.py:38
  7.9 104.2 %all-gather.9.cloned.1.call-start = ((), (), s32[]{:S(2)}) async-start(), calls=%async_computation.12 | async-start | bytes 2359296 | tf_op jit(solution)/shard_map/all_gather | solution.py:39
  8.6 143.0 %reduce-scatter.8.cloned.1.call-start = ((), (), s32[]{:S(2)}) async-start(), calls=%async_computation.7 | async-start | bytes 3932160 | tf_op jit(solution)/shard_map/reduce_scatter | solution.py:59
  64.6 57.4 %copy-start.9 = (bf16[8,96,1024]{2,1,0:T(8,128)(2,1)}, bf16[8,96,1024]{2,1,0:T(8,128)(2,1)S(1)}, u32[]{:S(2)}) copy-start(bf16[8,96,1024]{2,1,0:T(8,128)(2,1)S(1)} %convolution_convert_fusion.2) | copy-start | bytes 4718596
  65.2 60.5 %copy-start.7 = (bf16[8,96,1024]{2,1,0:T(8,128)(2,1)}, bf16[8,96,1024]{2,1,0:T(8,128)(2,1)S(1)}, u32[]{:S(2)}) copy-start(bf16[8,96,1024]{2,1,0:T(8,128)(2,1)S(1)} %convolution_convert_fusion.3) | copy-start | bytes 4718596
  71.6 120.9 %reduce-scatter.12.cloned.1.call-start = ((), (), s32[]{:S(2)}) async-start(), calls=%async_computation.9 | async-start | bytes 3932160 | tf_op jit(solution)/shard_map/reduce_scatter | solution.py:59
  121.5 111.9 %reduce-scatter.6.cloned.1.call-start = ((), (), s32[]{:S(2)}) async-start(), calls=%async_computation.6 | async-start | bytes 3932160 | tf_op jit(solution)/shard_map/reduce_scatter | solution.py:59
  129.5 260.1 %reduce-scatter.10.cloned.1.call-start = ((), (), s32[]{:S(2)}) async-start(), calls=%async_computation.8 | async-start | bytes 2359296 | tf_op jit(solution)/shard_map/reduce_scatter | solution.py:87
  151.7 90.1 %copy-start.4 = (bf16[384,1024]{1,0:T(8,128)(2,1)S(1)}, bf16[384,1024]{1,0:T(8,128)(2,1)}, u32[]{:S(2)}) copy-start(bf16[384,1024]{1,0:T(8,128)(2,1)} %reduce-scatter.8.cloned.1.call-done) | copy-start | bytes 2359300
  192.5 49.2 %copy-start.5 = (bf16[384,1024]{1,0:T(8,128)(2,1)S(1)}, bf16[384,1024]{1,0:T(8,128)(2,1)}, u32[]{:S(2)}) copy-start(bf16[384,1024]{1,0:T(8,128)(2,1)} %reduce-scatter.12.cloned.1.call-done) | copy-start | bytes 2359300
  244.1 62.0 %copy-start.3 = (bf16[384,1024]{1,0:T(8,128)(2,1)}, bf16[384,1024]{1,0:T(8,128)(2,1)S(1)}, u32[]{:S(2)}) copy-start(bf16[384,1024]{1,0:T(8,128)(2,1)S(1)} %get-tuple-element.16) | copy-start | bytes 2359300
  244.1 19.2 %collective-permute-start = (bf16[384,1024]{1,0:T(8,128)(2,1)S(1)}, bf16[384,1024]{1,0:T(8,128)(2,1)S(1)}, u32[]{:S(2)}, u32[]{:S(2)}) collective-permute-start(bf16[384,1024]{1,0:T(8,128)(2,1)S(1)} %get-tuple-element.16), channel_id=1, source_target_pairs={{0,1},{1,2},{2,3},{3,0},{4,5},{5,6},{6,7},{7,4},{8,9},{9,10},{10,1... | collective-permute-start | bytes 2359304 | tf_op jit(solution)/shard_map/ppermute | solution.py:71
  244.4 20.7 %collective-permute-start.2 = (bf16[384,1024]{1,0:T(8,128)(2,1)S(1)}, bf16[384,1024]{1,0:T(8,128)(2,1)S(1)}, u32[]{:S(2)}, u32[]{:S(2)}) collective-permute-start(bf16[384,1024]{1,0:T(8,128)(2,1)S(1)} %get-tuple-element.16), channel_id=1, source_target_pairs={{1,0},{2,1},{3,2},{0,3},{5,4},{6,5},{7,6},{4,7},{9,8},{10,9},{11,1... | collective-permute-start | bytes 2359304 | tf_op jit(solution)/shard_map/ppermute | solution.py:73
  245.8 33.2 %collective-permute-start.6 = (bf16[384,1024]{1,0:T(8,128)(2,1)}, bf16[384,1024]{1,0:T(8,128)(2,1)}, u32[]{:S(2)}, u32[]{:S(2)}) collective-permute-start(bf16[384,1024]{1,0:T(8,128)(2,1)} %get-tuple-element.15), channel_id=1, source_target_pairs={{0,1},{1,2},{2,3},{3,0},{4,5},{5,6},{6,7},{7,4},{8,9},{9,10},{10,1... | collective-permute-start | bytes 2359304 | tf_op jit(solution)/shard_map/ppermute | solution.py:71
  245.8 50.0 %collective-permute-start.3 = (bf16[384,1024]{1,0:T(8,128)(2,1)}, bf16[384,1024]{1,0:T(8,128)(2,1)}, u32[]{:S(2)}, u32[]{:S(2)}) collective-permute-start(bf16[384,1024]{1,0:T(8,128)(2,1)} %get-tuple-element.14), channel_id=1, source_target_pairs={{0,1},{1,2},{2,3},{3,0},{4,5},{5,6},{6,7},{7,4},{8,9},{9,10},{10,1... | collective-permute-start | bytes 2359304 | tf_op jit(solution)/shard_map/ppermute | solution.py:71
  263.3 42.8 %copy-start.27 = (bf16[384,1024]{1,0:T(8,128)(2,1)}, bf16[384,1024]{1,0:T(8,128)(2,1)S(1)}, u32[]{:S(2)}) copy-start(bf16[384,1024]{1,0:T(8,128)(2,1)S(1)} %collective-permute-done) | copy-start | bytes 2359300
  263.3 42.8 %collective-permute-start.1 = (bf16[384,1024]{1,0:T(8,128)(2,1)S(1)}, bf16[384,1024]{1,0:T(8,128)(2,1)S(1)}, u32[]{:S(2)}, u32[]{:S(2)}) collective-permute-start(bf16[384,1024]{1,0:T(8,128)(2,1)S(1)} %collective-permute-done), channel_id=1, source_target_pairs={{0,1},{1,2},{2,3},{3,0},{4,5},{5,6},{6,7},{7,4},{8,9},{9,10},{10,1... | collective-permute-start | bytes 2359304 | tf_op jit(solution)/shard_map/ppermute | solution.py:71
  263.3 58.0 %collective-permute-start.8 = (bf16[384,1024]{1,0:T(8,128)(2,1)}, bf16[384,1024]{1,0:T(8,128)(2,1)}, u32[]{:S(2)}, u32[]{:S(2)}) collective-permute-start(bf16[384,1024]{1,0:T(8,128)(2,1)} %get-tuple-element.15), channel_id=1, source_target_pairs={{1,0},{2,1},{3,2},{0,3},{5,4},{6,5},{7,6},{4,7},{9,8},{10,9},{11,1... | collective-permute-start | bytes 2359304 | tf_op jit(solution)/shard_map/ppermute | solution.py:73
  265.1 40.9 %copy-start.28 = (bf16[384,1024]{1,0:T(8,128)(2,1)}, bf16[384,1024]{1,0:T(8,128)(2,1)S(1)}, u32[]{:S(2)}) copy-start(bf16[384,1024]{1,0:T(8,128)(2,1)S(1)} %collective-permute-done.2) | copy-start | bytes 2359300
  265.1 62.1 %collective-permute-start.5 = (bf16[384,1024]{1,0:T(8,128)(2,1)}, bf16[384,1024]{1,0:T(8,128)(2,1)}, u32[]{:S(2)}, u32[]{:S(2)}) collective-permute-start(bf16[384,1024]{1,0:T(8,128)(2,1)} %get-tuple-element.14), channel_id=1, source_target_pairs={{1,0},{2,1},{3,2},{0,3},{5,4},{6,5},{7,6},{4,7},{9,8},{10,9},{11,1... | collective-permute-start | bytes 2359304 | tf_op jit(solution)/shard_map/ppermute | solution.py:73
  279.0 42.3 %collective-permute-start.7 = (bf16[384,1024]{1,0:T(8,128)(2,1)}, bf16[384,1024]{1,0:T(8,128)(2,1)}, u32[]{:S(2)}, u32[]{:S(2)}) collective-permute-start(bf16[384,1024]{1,0:T(8,128)(2,1)} %collective-permute-done.6), channel_id=1, source_target_pairs={{0,1},{1,2},{2,3},{3,0},{4,5},{5,6},{6,7},{7,4},{8,9},{9,10},{10,1... | collective-permute-start | bytes 2359304 | tf_op jit(solution)/shard_map/ppermute | solution.py:71
  295.8 31.4 %collective-permute-start.4 = (bf16[384,1024]{1,0:T(8,128)(2,1)}, bf16[384,1024]{1,0:T(8,128)(2,1)}, u32[]{:S(2)}, u32[]{:S(2)}) collective-permute-start(bf16[384,1024]{1,0:T(8,128)(2,1)} %collective-permute-done.3), channel_id=1, source_target_pairs={{0,1},{1,2},{2,3},{3,0},{4,5},{5,6},{6,7},{7,4},{8,9},{9,10},{10,1... | collective-permute-start | bytes 2359304 | tf_op jit(solution)/shard_map/ppermute | solution.py:71
  321.1 140.1 %reduce-scatter.14.cloned.1.call-start = ((), (), s32[]{:S(2)}) async-start(), calls=%async_computation.10 | async-start | bytes 2359296 | tf_op jit(solution)/shard_map/reduce_scatter | solution.py:87
  349.8 14.9 %copy-start.18 = (bf16[2,384,1024]{2,1,0:T(8,128)(2,1)S(1)}, bf16[2,384,1024]{2,1,0:T(8,128)(2,1)}, u32[]{:S(2)}) copy-start(bf16[2,384,1024]{2,1,0:T(8,128)(2,1)} %copy-done.17) | copy-start | bytes 4718596
  (29 other events, 117.5 us)
Sparse Core Ops, SparseCore 0:
  10.1 52.1 all-gather.6
  64.4 47.6 all-gather.8
  115.2 36.4 reduce-scatter.7
  154.6 37.8 reduce-scatter.11
  195.5 37.8 reduce-scatter.5
  321.2 68.3 reduce-scatter.9
  393.8 67.3 reduce-scatter.13
